TPU v7x, 1024 devices: a whole 4x8x16 slice. The times are simulated.
1024 devices in a mesh: theta: 64 (over z, y_lo, core), ax: 16 (over y_hi, x).
Axes of the slice: x: 4, y: 8 (y_hi: 4, y_lo: 2; y = y_hi * 2 + y_lo), z: 16, core: 2. Of those that a mesh axis runs over, the one named last changes fastest.
Arguments:
- adjoint_start: float32 [2, 5, 256, 128, 128], P(None, None, 'theta', 'ax'), may hold values from -6 to 6
- jacobian: bfloat16 [7, 5, 5, 256, 128, 128], P(None, None, None, 'theta', 'ax'), may hold values from -1 to 1
- objective_gradient: float32 [2, 5, 256, 128, 128], P(None, None, 'theta', 'ax'), may hold values from -6 to 6
- wall_mask: int32 [256, 128, 128], P('theta', 'ax'), may hold values 0 or 1
Outputs:
- adjoint_end: float32 [2, 5, 256, 128, 128], P(None, None, 'theta', 'ax')
All inputs are finite; a program needn't handle non-finite values. No bound on the sum of `wall_mask` on one device may be relied on, other than what follows from the above.
Results may differ from a plain program's by a relative error of at most 0.0003.
Values sent between devices are 32-bit elements; how exact they have to be, the bound alone decides.
A program may use at most 32 MiB of HBM per device.

v0:
```python
import jax
import jax.numpy as jnp
from jax import lax
from jax.sharding import PartitionSpec as P

SWEEPS = 3


step_size = 0.4
epsilon = 1e-06


def with_halo(value, sides, width):
    edges = {}
    for axis, dim in sides:
        size, length = (lax.axis_size(axis), value.shape[dim])
        up = [(i, (i + 1) % size) for i in range(size)]
        last = lax.slice_in_dim(value, length - width, length, axis=dim)
        leading = lax.slice_in_dim(value, 0, width, axis=dim)
        edges[dim] = (
            lax.ppermute(last, axis, up),
            lax.ppermute(leading, axis, [(b, a) for a, b in up]),
        )
    done = []
    for _, dim in sides:
        low, high = edges[dim]
        around = [(width, width) if d in done else (0, 0) for d in range(value.ndim)]
        value = jnp.concatenate([jnp.pad(low, around), value, jnp.pad(high, around)], axis=dim)
        done.append(dim)
    return value


def copy_for_each(value, axis):
    length = lax.axis_size(axis)
    return lax.all_to_all(
        jnp.broadcast_to(value[None], (length, *value.shape)), axis, 0, 0, tiled=True
    )


def of_everyone(value, axis):
    return copy_for_each(value, axis).sum(axis=0)


def exchange_rims(field):
    padded = with_halo(field, (("theta", 2), ("ax", 3)), 2)
    height = padded.shape[3]
    row_index = lax.broadcasted_iota(jnp.int32, (1, 1, 1, height, 1), 3)
    is_first = lax.axis_index("ax") == 0
    is_last = lax.axis_index("ax") == lax.axis_size("ax") - 1
    outside = jnp.logical_or(
        jnp.logical_and(is_first, row_index < 2), jnp.logical_and(is_last, row_index >= height - 2)
    )
    padded = jnp.where(outside, jnp.float32(0.0), padded)
    beside_all = padded[:, :, :, 2:-2]
    axial = padded[:, :, 2:-2, 1:-1]
    return (beside_all, axial)


def residual_of(adjoint, beside_all, axial, jac_float, objective_gradient, wall_mask):
    extent = adjoint.shape[2]
    neighbours = [
        adjoint,
        beside_all[:, :, 1 : extent + 1],
        beside_all[:, :, 3 : extent + 3],
        beside_all[:, :, 0:extent],
        beside_all[:, :, 4 : extent + 4],
        axial[:, :, :, :-2],
        axial[:, :, :, 2:],
    ]
    summed = -objective_gradient
    for offset in range(7):
        source = neighbours[offset]
        for inner in range(jac_float.shape[1]):
            summed = summed + jac_float[offset, inner][None] * source[:, inner][:, None]
    return jnp.where(wall_mask[None, None] == 1, jnp.float32(0.0), summed)


def norm_sum(partial_value):
    return of_everyone(of_everyone(partial_value, "ax"), "theta")


def per_device(adjoint_start, jacobian, objective_gradient, wall_mask):
    adjoint = adjoint_start
    jac_float = jacobian.astype(jnp.float32)
    cells = (
        adjoint.shape[1]
        * adjoint.shape[2]
        * adjoint.shape[3]
        * adjoint.shape[4]
        * lax.axis_size("theta")
        * lax.axis_size("ax")
    )
    beside_all, axial = exchange_rims(adjoint)
    for sweep_index in range(SWEEPS):
        summed = residual_of(adjoint, beside_all, axial, jac_float, objective_gradient, wall_mask)
        partial_value = jnp.sum(summed * summed, axis=(1, 2, 3, 4))
        if sweep_index + 1 < SWEEPS:
            res_around, res_axial = exchange_rims(summed)
        squares = norm_sum(partial_value)
        norm_value = jnp.sqrt(squares / cells + epsilon)[:, None, None, None, None]
        adjoint = adjoint - step_size * summed / norm_value
        if sweep_index + 1 < SWEEPS:
            beside_all = beside_all - step_size * res_around / norm_value
            axial = axial - step_size * res_axial / norm_value
    return adjoint


def solution(mesh):
    placed = (
        P(None, None, "theta", "ax", None),
        P(None, None, None, "theta", "ax", None),
        P(None, None, "theta", "ax", None),
        P("theta", "ax", None),
    )
    return jax.shard_map(
        per_device,
        mesh=mesh,
        in_specs=placed,
        out_specs=P(None, None, "theta", "ax", None),
        check_vma=False,
    )
```

profile of v0, /device:TPU:1, one launch (start us, length us, event | category | flops | bytes accessed | tf_op | source)
XLA Modules:
  0.0 184.9 jit_solution(10672677331496198020)
XLA Ops:
  0.0 0.9 fusion.15
  0.9 4.6 %collective-permute-start.1 = (f32[2,5,2,8,128]{4,3,2,1,0:T(8,128)S(1)}, f32[2,5,2,8,128]{4,3,2,1,0:T(8,128)}, u32[]{:S(2)}, u32[]{:S(2)}) collective-permute-start(f32[2,5,2,8,128]{4,3,2,1,0:T(8,128)S(1)} %get-tuple-element.157), channel_id=1, source_target_pairs={{0,16},{16,32},{32,48},{48,64},{64,80},{80,96},{96,112},{112,128},... | collective-permute-start | bytes 245768 | tf_op jit(solution)/shard_map/ppermute | solution.py:21
  5.5 13.4 %collective-permute-start.2 = (f32[2,5,2,8,128]{4,3,2,1,0:T(8,128)S(1)}, f32[2,5,2,8,128]{4,3,2,1,0:T(8,128)}, u32[]{:S(2)}, u32[]{:S(2)}) collective-permute-start(f32[2,5,2,8,128]{4,3,2,1,0:T(8,128)S(1)} %get-tuple-element.158), channel_id=1, source_target_pairs={{16,0},{32,16},{48,32},{64,48},{80,64},{96,80},{112,96},{128,112},... | collective-permute-start | bytes 245768 | tf_op jit(solution)/shard_map/ppermute | solution.py:22
  18.9 1.0 fusion.16
  19.9 1.9 %collective-permute-start = (f32[2,5,4,2,128]{4,3,2,1,0:T(2,128)S(1)}, f32[2,5,4,2,128]{4,3,2,1,0:T(2,128)}, u32[]{:S(2)}, u32[]{:S(2)}) collective-permute-start(f32[2,5,4,2,128]{4,3,2,1,0:T(2,128)S(1)} %get-tuple-element.159), channel_id=1, source_target_pairs={{0,1},{1,2},{2,3},{3,4},{4,5},{5,6},{6,7},{7,8},{8,9},{9,10},{10,1... | collective-permute-start | bytes 122888 | tf_op jit(solution)/shard_map/ppermute | solution.py:21
  21.9 7.6 %collective-permute-start.3 = (f32[2,5,4,2,128]{4,3,2,1,0:T(2,128)S(1)}, f32[2,5,4,2,128]{4,3,2,1,0:T(2,128)}, u32[]{:S(2)}, u32[]{:S(2)}) collective-permute-start(f32[2,5,4,2,128]{4,3,2,1,0:T(2,128)S(1)} %get-tuple-element.160), channel_id=1, source_target_pairs={{1,0},{2,1},{3,2},{4,3},{5,4},{6,5},{7,6},{8,7},{9,8},{10,9},{11,1... | collective-permute-start | bytes 122888 | tf_op jit(solution)/shard_map/ppermute | solution.py:22
  29.5 1.7 convert_element_type.10
  31.2 0.1 slice_bitcast_fusion.34
  31.4 0.8 slice_bitcast_fusion.33
  32.2 0.7 slice_bitcast_fusion.139
  33.1 0.6 and_or_fusion
  33.7 1.1 fusion.2
  35.1 0.9 multiply_reduce_fusion.2
  36.0 0.6 broadcast_in_dim.86
  36.6 4.3 %all-to-all-start = ((f32[16,1,2]{2,1,0:T(1,128)}), f32[16,1,2]{2,1,0:T(1,128)S(1)}, u32[]{:S(2)}, u32[]{:S(2)}) async-start(f32[16,1,2]{2,1,0:T(1,128)} %broadcast_in_dim.86), calls=%async_computation | async-start | bytes 16384 | tf_op jit(solution)/shard_map/all_to_all | solution.py:35
  41.0 8.8 %all-to-all-done = f32[16,1,2]{2,1,0:T(1,128)S(1)} async-done(((f32[16,1,2]{2,1,0:T(1,128)}), f32[16,1,2]{2,1,0:T(1,128)S(1)}, u32[]{:S(2)}, u32[]{:S(2)}) %all-to-all-start) | async-done | bytes 160 | tf_op jit(solution)/shard_map/all_to_all | solution.py:35
  49.8 0.6 broadcast_in_dim.87
  50.4 15.6 %all-to-all-start.1 = ((f32[64,1,2]{2,1,0:T(1,128)}), f32[64,1,2]{2,1,0:T(1,128)S(1)}, u32[]{:S(2)}, u32[]{:S(2)}) async-start(f32[64,1,2]{2,1,0:T(1,128)} %broadcast_in_dim.87), calls=%async_computation.1 | async-start | bytes 65536 | tf_op jit(solution)/shard_map/all_to_all | solution.py:35
  66.1 0.6 fusion.14
  66.7 3.5 %collective-permute-start.5 = (f32[2,5,2,8,128]{4,3,2,1,0:T(8,128)S(1)}, f32[2,5,2,8,128]{4,3,2,1,0:T(8,128)S(1)}, u32[]{:S(2)}, u32[]{:S(2)}) collective-permute-start(f32[2,5,2,8,128]{4,3,2,1,0:T(8,128)S(1)} %get-tuple-element.148), channel_id=1, source_target_pairs={{0,16},{16,32},{32,48},{48,64},{64,80},{80,96},{96,112},{112,128},... | collective-permute-start | bytes 245768 | tf_op jit(solution)/shard_map/ppermute | solution.py:21
  70.2 1.9 %collective-permute-start.6 = (f32[2,5,2,8,128]{4,3,2,1,0:T(8,128)S(1)}, f32[2,5,2,8,128]{4,3,2,1,0:T(8,128)}, u32[]{:S(2)}, u32[]{:S(2)}) collective-permute-start(f32[2,5,2,8,128]{4,3,2,1,0:T(8,128)S(1)} %get-tuple-element.149), channel_id=1, source_target_pairs={{16,0},{32,16},{48,32},{64,48},{80,64},{96,80},{112,96},{128,112},... | collective-permute-start | bytes 245768 | tf_op jit(solution)/shard_map/ppermute | solution.py:22
  72.2 2.0 %collective-permute-start.4 = (f32[2,5,4,2,128]{4,3,2,1,0:T(2,128)}, f32[2,5,4,2,128]{4,3,2,1,0:T(2,128)}, u32[]{:S(2)}, u32[]{:S(2)}) collective-permute-start(f32[2,5,4,2,128]{4,3,2,1,0:T(2,128)} %get-tuple-element.150), channel_id=1, source_target_pairs={{0,1},{1,2},{2,3},{3,4},{4,5},{5,6},{6,7},{7,8},{8,9},{9,10},{10,1... | collective-permute-start | bytes 122888 | tf_op jit(solution)/shard_map/ppermute | solution.py:21
  74.2 7.5 %collective-permute-start.7 = (f32[2,5,4,2,128]{4,3,2,1,0:T(2,128)S(1)}, f32[2,5,4,2,128]{4,3,2,1,0:T(2,128)}, u32[]{:S(2)}, u32[]{:S(2)}) collective-permute-start(f32[2,5,4,2,128]{4,3,2,1,0:T(2,128)S(1)} %get-tuple-element.151), channel_id=1, source_target_pairs={{1,0},{2,1},{3,2},{4,3},{5,4},{6,5},{7,6},{8,7},{9,8},{10,9},{11,1... | collective-permute-start | bytes 122888 | tf_op jit(solution)/shard_map/ppermute | solution.py:22
  82.1 0.7 collective-permute-done.7
  82.8 1.1 fusion.1
  83.9 0.1 fusion.10
  84.0 0.1 fusion.8
  84.4 0.9 multiply_reduce_fusion.1
  85.3 0.6 broadcast_in_dim.88
  85.9 7.5 %all-to-all-start.2 = ((f32[16,1,2]{2,1,0:T(1,128)}), f32[16,1,2]{2,1,0:T(1,128)S(1)}, u32[]{:S(2)}, u32[]{:S(2)}) async-start(f32[16,1,2]{2,1,0:T(1,128)} %broadcast_in_dim.88), calls=%async_computation.2 | async-start | bytes 16384 | tf_op jit(solution)/shard_map/all_to_all | solution.py:35
  93.3 0.7 fusion.11
  94.0 8.2 %all-to-all-done.2 = f32[16,1,2]{2,1,0:T(1,128)S(1)} async-done(((f32[16,1,2]{2,1,0:T(1,128)}), f32[16,1,2]{2,1,0:T(1,128)S(1)}, u32[]{:S(2)}, u32[]{:S(2)}) %all-to-all-start.2) | async-done | bytes 160 | tf_op jit(solution)/shard_map/all_to_all | solution.py:35
  102.2 0.6 broadcast_in_dim.89
  102.8 17.7 %all-to-all-start.3 = ((f32[64,1,2]{2,1,0:T(1,128)}), f32[64,1,2]{2,1,0:T(1,128)S(1)}, u32[]{:S(2)}, u32[]{:S(2)}) async-start(f32[64,1,2]{2,1,0:T(1,128)} %broadcast_in_dim.89), calls=%async_computation.3 | async-start | bytes 65536 | tf_op jit(solution)/shard_map/all_to_all | solution.py:35
  120.6 0.7 fusion.12
  121.3 2.4 %collective-permute-start.10 = (f32[2,5,2,8,128]{4,3,2,1,0:T(8,128)}, f32[2,5,2,8,128]{4,3,2,1,0:T(8,128)}, u32[]{:S(2)}, u32[]{:S(2)}) collective-permute-start(f32[2,5,2,8,128]{4,3,2,1,0:T(8,128)} %get-tuple-element.140), channel_id=1, source_target_pairs={{16,0},{32,16},{48,32},{64,48},{80,64},{96,80},{112,96},{128,112},... | collective-permute-start | bytes 245768 | tf_op jit(solution)/shard_map/ppermute | solution.py:22
  123.6 3.2 %collective-permute-start.9 = (f32[2,5,2,8,128]{4,3,2,1,0:T(8,128)}, f32[2,5,2,8,128]{4,3,2,1,0:T(8,128)}, u32[]{:S(2)}, u32[]{:S(2)}) collective-permute-start(f32[2,5,2,8,128]{4,3,2,1,0:T(8,128)} %get-tuple-element.139), channel_id=1, source_target_pairs={{0,16},{16,32},{32,48},{48,64},{64,80},{80,96},{96,112},{112,128},... | collective-permute-start | bytes 245768 | tf_op jit(solution)/shard_map/ppermute | solution.py:21
  126.8 2.8 %collective-permute-start.11 = (f32[2,5,4,2,128]{4,3,2,1,0:T(2,128)}, f32[2,5,4,2,128]{4,3,2,1,0:T(2,128)}, u32[]{:S(2)}, u32[]{:S(2)}) collective-permute-start(f32[2,5,4,2,128]{4,3,2,1,0:T(2,128)} %get-tuple-element.142), channel_id=1, source_target_pairs={{1,0},{2,1},{3,2},{4,3},{5,4},{6,5},{7,6},{8,7},{9,8},{10,9},{11,1... | collective-permute-start | bytes 122888 | tf_op jit(solution)/shard_map/ppermute | solution.py:22
  129.7 2.5 %collective-permute-start.8 = (f32[2,5,4,2,128]{4,3,2,1,0:T(2,128)}, f32[2,5,4,2,128]{4,3,2,1,0:T(2,128)}, u32[]{:S(2)}, u32[]{:S(2)}) collective-permute-start(f32[2,5,4,2,128]{4,3,2,1,0:T(2,128)} %get-tuple-element.141), channel_id=1, source_target_pairs={{0,1},{1,2},{2,3},{3,4},{4,5},{5,6},{6,7},{7,8},{8,9},{9,10},{10,1... | collective-permute-start | bytes 122888 | tf_op jit(solution)/shard_map/ppermute | solution.py:21
  132.1 1.7 all-to-all-done.3
  134.1 5.2 %collective-permute-done.8 = f32[2,5,4,2,128]{4,3,2,1,0:T(2,128)} collective-permute-done((f32[2,5,4,2,128]{4,3,2,1,0:T(2,128)}, f32[2,5,4,2,128]{4,3,2,1,0:T(2,128)}, u32[]{:S(2)}, u32[]{:S(2)}) %collective-permute-start.8) | collective-permute-done | bytes 40992 | tf_op jit(solution)/shard_map/ppermute | solution.py:21
  139.3 1.1 fusion
  140.5 0.1 fusion.6
  140.7 0.1 fusion.4
  140.9 0.9 multiply_reduce_fusion
  141.8 12.9 %all_to_all.36 = f32[16,1,2]{2,1,0:T(1,128)S(1)} all-to-all(f32[16,1,2]{2,1,0:T(1,128)S(1)} %broadcast_in_dim.90), channel_id=1, replica_groups=mesh['theta'=64,'ax'=16] {'ax'}, dimensions={0} | all-to-all | bytes 256 | tf_op jit(solution)/shard_map/all_to_all | solution.py:35
  154.8 29.2 %all_to_all.37 = f32[64,1,2]{2,1,0:T(1,128)S(1)} all-to-all(f32[64,1,2]{2,1,0:T(1,128)S(1)} %broadcast_in_dim.91), channel_id=1, replica_groups=mesh['theta'=64,'ax'=16] {'theta'}, dimensions={0} | all-to-all | bytes 1024 | tf_op jit(solution)/shard_map/all_to_all | solution.py:35
  184.1 0.8 divide_subtract_fusion
  (125 shorter events, 1.2 us)
Async XLA Ops:
  0.9 32.7 %collective-permute-start.1 = (f32[2,5,2,8,128]{4,3,2,1,0:T(8,128)S(1)}, f32[2,5,2,8,128]{4,3,2,1,0:T(8,128)}, u32[]{:S(2)}, u32[]{:S(2)}) collective-permute-start(f32[2,5,2,8,128]{4,3,2,1,0:T(8,128)S(1)} %get-tuple-element.157), channel_id=1, source_target_pairs={{0,16},{16,32},{32,48},{48,64},{64,80},{80,96},{96,112},{112,128},... | collective-permute-start | bytes 245768 | tf_op jit(solution)/shard_map/ppermute | solution.py:21
  5.5 28.1 %collective-permute-start.2 = (f32[2,5,2,8,128]{4,3,2,1,0:T(8,128)S(1)}, f32[2,5,2,8,128]{4,3,2,1,0:T(8,128)}, u32[]{:S(2)}, u32[]{:S(2)}) collective-permute-start(f32[2,5,2,8,128]{4,3,2,1,0:T(8,128)S(1)} %get-tuple-element.158), channel_id=1, source_target_pairs={{16,0},{32,16},{48,32},{64,48},{80,64},{96,80},{112,96},{128,112},... | collective-permute-start | bytes 245768 | tf_op jit(solution)/shard_map/ppermute | solution.py:22
  19.9 13.7 %collective-permute-start = (f32[2,5,4,2,128]{4,3,2,1,0:T(2,128)S(1)}, f32[2,5,4,2,128]{4,3,2,1,0:T(2,128)}, u32[]{:S(2)}, u32[]{:S(2)}) collective-permute-start(f32[2,5,4,2,128]{4,3,2,1,0:T(2,128)S(1)} %get-tuple-element.159), channel_id=1, source_target_pairs={{0,1},{1,2},{2,3},{3,4},{4,5},{5,6},{6,7},{7,8},{8,9},{9,10},{10,1... | collective-permute-start | bytes 122888 | tf_op jit(solution)/shard_map/ppermute | solution.py:21
  21.9 11.8 %collective-permute-start.3 = (f32[2,5,4,2,128]{4,3,2,1,0:T(2,128)S(1)}, f32[2,5,4,2,128]{4,3,2,1,0:T(2,128)}, u32[]{:S(2)}, u32[]{:S(2)}) collective-permute-start(f32[2,5,4,2,128]{4,3,2,1,0:T(2,128)S(1)} %get-tuple-element.160), channel_id=1, source_target_pairs={{1,0},{2,1},{3,2},{4,3},{5,4},{6,5},{7,6},{8,7},{9,8},{10,9},{11,1... | collective-permute-start | bytes 122888 | tf_op jit(solution)/shard_map/ppermute | solution.py:22
  31.4 3.6 %copy-start.1 = (f32[2,5,4,8,128]{4,3,2,1,0:T(8,128)S(1)}, f32[2,5,4,8,128]{4,3,2,1,0:T(8,128)}, u32[]{:S(2)}) copy-start(f32[2,5,4,8,128]{4,3,2,1,0:T(8,128)} %param.6) | copy-start | bytes 491524
  32.2 3.8 %copy-start.2 = (f32[5,4,8,128]{3,2,1,0:T(8,128)}, f32[5,4,8,128]{3,2,1,0:T(8,128)S(1)}, u32[]{:S(2)}) copy-start(f32[5,4,8,128]{3,2,1,0:T(8,128)S(1)} %get-tuple-element.34) | copy-start | bytes 245764
  32.2 3.8 %copy-start.5 = (f32[5,4,8,128]{3,2,1,0:T(8,128)}, f32[5,4,8,128]{3,2,1,0:T(8,128)S(1)}, u32[]{:S(2)}) copy-start(f32[5,4,8,128]{3,2,1,0:T(8,128)S(1)} %get-tuple-element.35) | copy-start | bytes 245764
  32.2 3.8 %copy-start.8 = (f32[5,4,8,128]{3,2,1,0:T(8,128)}, f32[5,4,8,128]{3,2,1,0:T(8,128)S(1)}, u32[]{:S(2)}) copy-start(f32[5,4,8,128]{3,2,1,0:T(8,128)S(1)} %get-tuple-element.36) | copy-start | bytes 245764
  32.2 3.8 %copy-start.11 = (f32[5,4,8,128]{3,2,1,0:T(8,128)}, f32[5,4,8,128]{3,2,1,0:T(8,128)S(1)}, u32[]{:S(2)}) copy-start(f32[5,4,8,128]{3,2,1,0:T(8,128)S(1)} %get-tuple-element.37) | copy-start | bytes 245764
  32.2 3.8 %copy-start.14 = (f32[5,4,8,128]{3,2,1,0:T(8,128)}, f32[5,4,8,128]{3,2,1,0:T(8,128)S(1)}, u32[]{:S(2)}) copy-start(f32[5,4,8,128]{3,2,1,0:T(8,128)S(1)} %get-tuple-element.38) | copy-start | bytes 245764
  32.2 3.8 %copy-start.17 = (f32[5,4,8,128]{3,2,1,0:T(8,128)}, f32[5,4,8,128]{3,2,1,0:T(8,128)S(1)}, u32[]{:S(2)}) copy-start(f32[5,4,8,128]{3,2,1,0:T(8,128)S(1)} %get-tuple-element.39) | copy-start | bytes 245764
  33.1 3.0 %copy-start.42 = (pred[4,8,128]{2,1,0:T(8,128)(4,1)}, pred[4,8,128]{2,1,0:T(8,128)(4,1)S(1)}, u32[]{:S(2)}) copy-start(pred[4,8,128]{2,1,0:T(8,128)(4,1)S(1)} %broadcast_compare_fusion) | copy-start | bytes 12292
  36.6 13.1 %all-to-all-start = ((f32[16,1,2]{2,1,0:T(1,128)}), f32[16,1,2]{2,1,0:T(1,128)S(1)}, u32[]{:S(2)}, u32[]{:S(2)}) async-start(f32[16,1,2]{2,1,0:T(1,128)} %broadcast_in_dim.86), calls=%async_computation | async-start | bytes 16384 | tf_op jit(solution)/shard_map/all_to_all | solution.py:35
  50.4 31.3 %all-to-all-start.1 = ((f32[64,1,2]{2,1,0:T(1,128)}), f32[64,1,2]{2,1,0:T(1,128)S(1)}, u32[]{:S(2)}, u32[]{:S(2)}) async-start(f32[64,1,2]{2,1,0:T(1,128)} %broadcast_in_dim.87), calls=%async_computation.1 | async-start | bytes 65536 | tf_op jit(solution)/shard_map/all_to_all | solution.py:35
  66.7 16.1 %collective-permute-start.5 = (f32[2,5,2,8,128]{4,3,2,1,0:T(8,128)S(1)}, f32[2,5,2,8,128]{4,3,2,1,0:T(8,128)S(1)}, u32[]{:S(2)}, u32[]{:S(2)}) collective-permute-start(f32[2,5,2,8,128]{4,3,2,1,0:T(8,128)S(1)} %get-tuple-element.148), channel_id=1, source_target_pairs={{0,16},{16,32},{32,48},{48,64},{64,80},{80,96},{96,112},{112,128},... | collective-permute-start | bytes 245768 | tf_op jit(solution)/shard_map/ppermute | solution.py:21
  70.2 12.5 %collective-permute-start.6 = (f32[2,5,2,8,128]{4,3,2,1,0:T(8,128)S(1)}, f32[2,5,2,8,128]{4,3,2,1,0:T(8,128)}, u32[]{:S(2)}, u32[]{:S(2)}) collective-permute-start(f32[2,5,2,8,128]{4,3,2,1,0:T(8,128)S(1)} %get-tuple-element.149), channel_id=1, source_target_pairs={{16,0},{32,16},{48,32},{64,48},{80,64},{96,80},{112,96},{128,112},... | collective-permute-start | bytes 245768 | tf_op jit(solution)/shard_map/ppermute | solution.py:22
  72.2 9.9 %collective-permute-start.4 = (f32[2,5,4,2,128]{4,3,2,1,0:T(2,128)}, f32[2,5,4,2,128]{4,3,2,1,0:T(2,128)}, u32[]{:S(2)}, u32[]{:S(2)}) collective-permute-start(f32[2,5,4,2,128]{4,3,2,1,0:T(2,128)} %get-tuple-element.150), channel_id=1, source_target_pairs={{0,1},{1,2},{2,3},{3,4},{4,5},{5,6},{6,7},{7,8},{8,9},{9,10},{10,1... | collective-permute-start | bytes 122888 | tf_op jit(solution)/shard_map/ppermute | solution.py:21
  74.2 8.6 %collective-permute-start.7 = (f32[2,5,4,2,128]{4,3,2,1,0:T(2,128)S(1)}, f32[2,5,4,2,128]{4,3,2,1,0:T(2,128)}, u32[]{:S(2)}, u32[]{:S(2)}) collective-permute-start(f32[2,5,4,2,128]{4,3,2,1,0:T(2,128)S(1)} %get-tuple-element.151), channel_id=1, source_target_pairs={{1,0},{2,1},{3,2},{4,3},{5,4},{6,5},{7,6},{8,7},{9,8},{10,9},{11,1... | collective-permute-start | bytes 122888 | tf_op jit(solution)/shard_map/ppermute | solution.py:22
  81.8 2.4 %copy-start.6 = (f32[5,4,8,128]{3,2,1,0:T(8,128)S(1)}, f32[5,4,8,128]{3,2,1,0:T(8,128)}, u32[]{:S(2)}) copy-start(f32[5,4,8,128]{3,2,1,0:T(8,128)} %copy-done.5) | copy-start | bytes 245764
  81.8 2.4 %copy-start.9 = (f32[5,4,8,128]{3,2,1,0:T(8,128)S(1)}, f32[5,4,8,128]{3,2,1,0:T(8,128)}, u32[]{:S(2)}) copy-start(f32[5,4,8,128]{3,2,1,0:T(8,128)} %copy-done.8) | copy-start | bytes 245764
  81.8 2.4 %copy-start.12 = (f32[5,4,8,128]{3,2,1,0:T(8,128)S(1)}, f32[5,4,8,128]{3,2,1,0:T(8,128)}, u32[]{:S(2)}) copy-start(f32[5,4,8,128]{3,2,1,0:T(8,128)} %copy-done.11) | copy-start | bytes 245764
  81.8 2.4 %copy-start.15 = (f32[5,4,8,128]{3,2,1,0:T(8,128)S(1)}, f32[5,4,8,128]{3,2,1,0:T(8,128)}, u32[]{:S(2)}) copy-start(f32[5,4,8,128]{3,2,1,0:T(8,128)} %copy-done.14) | copy-start | bytes 245764
  81.8 2.4 %copy-start.18 = (f32[5,4,8,128]{3,2,1,0:T(8,128)S(1)}, f32[5,4,8,128]{3,2,1,0:T(8,128)}, u32[]{:S(2)}) copy-start(f32[5,4,8,128]{3,2,1,0:T(8,128)} %copy-done.17) | copy-start | bytes 245764
  81.9 2.4 %copy-start.21 = (f32[5,4,8,128]{3,2,1,0:T(8,128)S(1)}, f32[5,4,8,128]{3,2,1,0:T(8,128)}, u32[]{:S(2)}) copy-start(f32[5,4,8,128]{3,2,1,0:T(8,128)} %get-tuple-element.40) | copy-start | bytes 245764
  81.9 2.4 %copy-start.24 = (f32[5,4,8,128]{3,2,1,0:T(8,128)S(1)}, f32[5,4,8,128]{3,2,1,0:T(8,128)}, u32[]{:S(2)}) copy-start(f32[5,4,8,128]{3,2,1,0:T(8,128)} %get-tuple-element.41) | copy-start | bytes 245764
  81.9 2.4 %copy-start.27 = (f32[5,4,8,128]{3,2,1,0:T(8,128)S(1)}, f32[5,4,8,128]{3,2,1,0:T(8,128)}, u32[]{:S(2)}) copy-start(f32[5,4,8,128]{3,2,1,0:T(8,128)} %get-tuple-element.42) | copy-start | bytes 245764
  81.9 2.4 %copy-start.30 = (f32[5,4,8,128]{3,2,1,0:T(8,128)S(1)}, f32[5,4,8,128]{3,2,1,0:T(8,128)}, u32[]{:S(2)}) copy-start(f32[5,4,8,128]{3,2,1,0:T(8,128)} %get-tuple-element.43) | copy-start | bytes 245764
  81.9 2.4 %copy-start.33 = (f32[5,4,8,128]{3,2,1,0:T(8,128)S(1)}, f32[5,4,8,128]{3,2,1,0:T(8,128)}, u32[]{:S(2)}) copy-start(f32[5,4,8,128]{3,2,1,0:T(8,128)} %get-tuple-element.44) | copy-start | bytes 245764
  81.9 2.4 %copy-start.36 = (f32[5,4,8,128]{3,2,1,0:T(8,128)S(1)}, f32[5,4,8,128]{3,2,1,0:T(8,128)}, u32[]{:S(2)}) copy-start(f32[5,4,8,128]{3,2,1,0:T(8,128)} %get-tuple-element.45) | copy-start | bytes 245764
  81.9 2.4 %copy-start.43 = (pred[4,8,128]{2,1,0:T(8,128)(4,1)S(1)}, pred[4,8,128]{2,1,0:T(8,128)(4,1)}, u32[]{:S(2)}) copy-start(pred[4,8,128]{2,1,0:T(8,128)(4,1)} %copy-done.42) | copy-start | bytes 12292
  85.9 16.3 %all-to-all-start.2 = ((f32[16,1,2]{2,1,0:T(1,128)}), f32[16,1,2]{2,1,0:T(1,128)S(1)}, u32[]{:S(2)}, u32[]{:S(2)}) async-start(f32[16,1,2]{2,1,0:T(1,128)} %broadcast_in_dim.88), calls=%async_computation.2 | async-start | bytes 16384 | tf_op jit(solution)/shard_map/all_to_all | solution.py:35
  102.8 31.0 %all-to-all-start.3 = ((f32[64,1,2]{2,1,0:T(1,128)}), f32[64,1,2]{2,1,0:T(1,128)S(1)}, u32[]{:S(2)}, u32[]{:S(2)}) async-start(f32[64,1,2]{2,1,0:T(1,128)} %broadcast_in_dim.89), calls=%async_computation.3 | async-start | bytes 65536 | tf_op jit(solution)/shard_map/all_to_all | solution.py:35
  121.3 18.1 %collective-permute-start.10 = (f32[2,5,2,8,128]{4,3,2,1,0:T(8,128)}, f32[2,5,2,8,128]{4,3,2,1,0:T(8,128)}, u32[]{:S(2)}, u32[]{:S(2)}) collective-permute-start(f32[2,5,2,8,128]{4,3,2,1,0:T(8,128)} %get-tuple-element.140), channel_id=1, source_target_pairs={{16,0},{32,16},{48,32},{64,48},{80,64},{96,80},{112,96},{128,112},... | collective-permute-start | bytes 245768 | tf_op jit(solution)/shard_map/ppermute | solution.py:22
  123.6 15.7 %collective-permute-start.9 = (f32[2,5,2,8,128]{4,3,2,1,0:T(8,128)}, f32[2,5,2,8,128]{4,3,2,1,0:T(8,128)}, u32[]{:S(2)}, u32[]{:S(2)}) collective-permute-start(f32[2,5,2,8,128]{4,3,2,1,0:T(8,128)} %get-tuple-element.139), channel_id=1, source_target_pairs={{0,16},{16,32},{32,48},{48,64},{64,80},{80,96},{96,112},{112,128},... | collective-permute-start | bytes 245768 | tf_op jit(solution)/shard_map/ppermute | solution.py:21
  126.8 7.3 %collective-permute-start.11 = (f32[2,5,4,2,128]{4,3,2,1,0:T(2,128)}, f32[2,5,4,2,128]{4,3,2,1,0:T(2,128)}, u32[]{:S(2)}, u32[]{:S(2)}) collective-permute-start(f32[2,5,4,2,128]{4,3,2,1,0:T(2,128)} %get-tuple-element.142), channel_id=1, source_target_pairs={{1,0},{2,1},{3,2},{4,3},{5,4},{6,5},{7,6},{8,7},{9,8},{10,9},{11,1... | collective-permute-start | bytes 122888 | tf_op jit(solution)/shard_map/ppermute | solution.py:22
  129.7 9.7 %collective-permute-start.8 = (f32[2,5,4,2,128]{4,3,2,1,0:T(2,128)}, f32[2,5,4,2,128]{4,3,2,1,0:T(2,128)}, u32[]{:S(2)}, u32[]{:S(2)}) collective-permute-start(f32[2,5,4,2,128]{4,3,2,1,0:T(2,128)} %get-tuple-element.141), channel_id=1, source_target_pairs={{0,1},{1,2},{2,3},{3,4},{4,5},{5,6},{6,7},{7,8},{8,9},{9,10},{10,1... | collective-permute-start | bytes 122888 | tf_op jit(solution)/shard_map/ppermute | solution.py:21
  133.9 6.9 %copy-start.4 = (f32[5,4,8,128]{3,2,1,0:T(8,128)S(1)}, f32[5,4,8,128]{3,2,1,0:T(8,128)}, u32[]{:S(2)}) copy-start(f32[5,4,8,128]{3,2,1,0:T(8,128)} %copy-done.2) | copy-start | bytes 245764
  133.9 6.9 %copy-start.7 = (f32[5,4,8,128]{3,2,1,0:T(8,128)S(1)}, f32[5,4,8,128]{3,2,1,0:T(8,128)}, u32[]{:S(2)}) copy-start(f32[5,4,8,128]{3,2,1,0:T(8,128)} %copy-done.5) | copy-start | bytes 245764
  133.9 6.9 %copy-start.10 = (f32[5,4,8,128]{3,2,1,0:T(8,128)S(1)}, f32[5,4,8,128]{3,2,1,0:T(8,128)}, u32[]{:S(2)}) copy-start(f32[5,4,8,128]{3,2,1,0:T(8,128)} %copy-done.8) | copy-start | bytes 245764
  133.9 6.9 %copy-start.13 = (f32[5,4,8,128]{3,2,1,0:T(8,128)S(1)}, f32[5,4,8,128]{3,2,1,0:T(8,128)}, u32[]{:S(2)}) copy-start(f32[5,4,8,128]{3,2,1,0:T(8,128)} %copy-done.11) | copy-start | bytes 245764
  133.9 6.9 %copy-start.16 = (f32[5,4,8,128]{3,2,1,0:T(8,128)S(1)}, f32[5,4,8,128]{3,2,1,0:T(8,128)}, u32[]{:S(2)}) copy-start(f32[5,4,8,128]{3,2,1,0:T(8,128)} %copy-done.14) | copy-start | bytes 245764
  133.9 6.9 %copy-start.19 = (f32[5,4,8,128]{3,2,1,0:T(8,128)S(1)}, f32[5,4,8,128]{3,2,1,0:T(8,128)}, u32[]{:S(2)}) copy-start(f32[5,4,8,128]{3,2,1,0:T(8,128)} %copy-done.17) | copy-start | bytes 245764
  134.0 6.9 %copy-start.22 = (f32[5,4,8,128]{3,2,1,0:T(8,128)S(1)}, f32[5,4,8,128]{3,2,1,0:T(8,128)}, u32[]{:S(2)}) copy-start(f32[5,4,8,128]{3,2,1,0:T(8,128)} %get-tuple-element.40) | copy-start | bytes 245764
  134.0 6.9 %copy-start.25 = (f32[5,4,8,128]{3,2,1,0:T(8,128)S(1)}, f32[5,4,8,128]{3,2,1,0:T(8,128)}, u32[]{:S(2)}) copy-start(f32[5,4,8,128]{3,2,1,0:T(8,128)} %get-tuple-element.41) | copy-start | bytes 245764
  134.0 6.9 %copy-start.28 = (f32[5,4,8,128]{3,2,1,0:T(8,128)S(1)}, f32[5,4,8,128]{3,2,1,0:T(8,128)}, u32[]{:S(2)}) copy-start(f32[5,4,8,128]{3,2,1,0:T(8,128)} %get-tuple-element.42) | copy-start | bytes 245764
  134.0 6.9 %copy-start.31 = (f32[5,4,8,128]{3,2,1,0:T(8,128)S(1)}, f32[5,4,8,128]{3,2,1,0:T(8,128)}, u32[]{:S(2)}) copy-start(f32[5,4,8,128]{3,2,1,0:T(8,128)} %get-tuple-element.43) | copy-start | bytes 245764
  134.0 6.9 %copy-start.34 = (f32[5,4,8,128]{3,2,1,0:T(8,128)S(1)}, f32[5,4,8,128]{3,2,1,0:T(8,128)}, u32[]{:S(2)}) copy-start(f32[5,4,8,128]{3,2,1,0:T(8,128)} %get-tuple-element.44) | copy-start | bytes 245764
  134.0 6.9 %copy-start.37 = (f32[5,4,8,128]{3,2,1,0:T(8,128)S(1)}, f32[5,4,8,128]{3,2,1,0:T(8,128)}, u32[]{:S(2)}) copy-start(f32[5,4,8,128]{3,2,1,0:T(8,128)} %get-tuple-element.45) | copy-start | bytes 245764
  (13 other events, 25.3 us)
where the time goes:
time: 186 us; the launch traced here: 185 us
  starting transfers between devices  98.4 us (53%)
  blocking collectives  42.1 us (23%)
  waiting for transfers between devices  24.6 us (13%)
  other arithmetic  10.2 us (5%)
  local copies, waits for them, and re-layouts  8.61 us (5%)
    all_to_all x4, starting transfers between devices, copy_for_each(): lax.all_to_all(jnp.broadcast_to(value[None], (length, *value.shape)), axi...  45.1 us
    all_to_all x2, blocking collectives, copy_for_each(): lax.all_to_all(jnp.broadcast_to(value[None], (length, *value.shape)), axi...  42.1 us
    ppermute x6, starting transfers between devices, with_halo(): lax.ppermute(leading, axis, [(b, a) for a, b in up])  35.5 us
    all_to_all x4, waiting for transfers between devices, copy_for_each(): lax.all_to_all(jnp.broadcast_to(value[None], (length, *value.shape)), axi...  18.7 us
    ppermute x6, starting transfers between devices, with_halo(): lax.ppermute(last, axis, up)  17.7 us
    ppermute x6, waiting for transfers between devices, with_halo(): lax.ppermute(last, axis, up)  5.21 us
    slice x6, local copies, waits for them, and re-layouts, with_halo(): last = lax.slice_in_dim(value, length - width, length, axis=dim)  3.96 us
  transfers between devices with their start and end apart: 16, of which 5 were waited for; matrix products, arithmetic and copies ran while one was open for 4% of the time, Pallas kernels for 0%

commit v1 on v0

v1 whole, which is shorter than its diff:
```python
import functools

import jax
import jax.numpy as jnp
from jax import lax
from jax.experimental import pallas as pl
from jax.experimental.pallas import tpu as pltpu
from jax.sharding import PartitionSpec as P

MESH = pl.DeviceIdType.MESH
F32 = jnp.float32
SWEEPS = 3
OBJ = 2
COMP = 5
NT = 4
STEP = 0.4
EPS = 1e-06
SHIFT = (0, -1, 1, -2, 2)

X = 4
YL = 2
CORES = 2


def near_last(size):
    return sorted(range(1, size), key=lambda d: -min(d, size - d))


def peer(n_theta, n_ax, dx=0, dy=0, dz=0, dc=0):
    theta, ax = lax.axis_index("theta"), lax.axis_index("ax")
    nz, ny = n_theta // (YL * CORES), (n_ax // X) * YL
    if dz:
        theta = (theta + YL * CORES * dz) % n_theta
    if dx:
        ax = (ax // X) * X + (ax % X + dx) % X
    if dc:
        theta = (theta // CORES) * CORES + (theta % CORES + dc) % CORES
    if dy:
        y_lo = (theta // CORES) % YL
        y = ((ax // X) * YL + y_lo + dy) % ny
        ax = (y // YL) * X + ax % X
        theta = theta + (y % YL - y_lo) * CORES
    return theta, ax


def stages(n_theta, n_ax):
    nz, ny = n_theta // (YL * CORES), (n_ax // X) * YL
    pairs = [(dx, dc) for dx in range(X) for dc in range(CORES) if dx or dc]
    pairs.sort(key=lambda p: (-min(p[0], X - p[0]), p[1]))
    return (
        [dict(dx=dx, dc=dc) for dx, dc in pairs],
        [dict(dy=dy) for dy in near_last(ny)],
        [dict(dz=dz) for dz in near_last(nz)],
    )


def two_sum(a, b):
    s = a + b
    bb = s - a
    return s, (a - (s - bb)) + (b - bb)


def fast_two_sum(a, b):
    s = a + b
    return s, b - (s - a)


def split(a):
    c = a * F32(4097.0)
    hi = c - (c - a)
    return hi, a - hi


def two_prod(a, sa, b, sb):
    p = a * b
    return p, ((sa[0] * sb[0] - p) + sa[0] * sb[1] + sa[1] * sb[0]) + sa[1] * sb[1]


def pair_add(a, b):
    s, e = two_sum(a[0], b[0])
    return s, e + (a[1] + b[1])


def norm_pair(a):
    return fast_two_sum(a[0], a[1])


def pair_mul(a, b):
    p, e = two_prod(a[0], split(a[0]), b[0], split(b[0]))
    return fast_two_sum(p, e + (a[0] * b[1] + a[1] * b[0]))


def scaled(a, k):
    return a[0] * F32(k), a[1] * F32(k)


def roll(x, shift, axis):
    return pltpu.roll(x, shift % x.shape[axis], axis)


def fold_rows(parts, sub):
    for k in (4, 2, 1):
        half = len(parts) // 2
        first = (sub // k) % 2 == 0
        merged = []
        for i in range(half):
            a, b = parts[i], parts[i + half]
            low = tuple(jnp.where(first, u, roll(v, k, 0)) for u, v in zip(a, b))
            high = tuple(jnp.where(first, roll(u, 8 - k, 0), v) for u, v in zip(a, b))
            merged.append(pair_add(low, high))
        parts = merged
    return parts[0]


def fold_lanes(part):
    for k in (64, 32, 16, 8, 4, 2, 1):
        part = pair_add(part, tuple(roll(v, k, 1) for v in part))
    return norm_pair(part)


def kernel(n_theta, n_ax, a_hbm, j_hbm, g_hbm, w_hbm, out_ref,
           fld, axs, axh, jb, jf, gb, wb, early, msg, got0, got1, got2,
           in_sem, send_sem, recv_sem, ar_send, ar_recv):
    theta, ax = lax.axis_index("theta"), lax.axis_index("ax")
    around = [
        ((theta + n_theta - 1) % n_theta, ax),
        ((theta + 1) % n_theta, ax),
        (theta, (ax + n_ax - 1) % n_ax),
        (theta, (ax + 1) % n_ax),
    ]
    levels = stages(n_theta, n_ax)
    barrier = pltpu.get_barrier_semaphore()
    greeted = around + [peer(n_theta, n_ax, **p) for level in reversed(levels) for p in level]
    for dev in greeted:
        pl.semaphore_signal(barrier, inc=1, device_id=dev, device_id_type=MESH)

    loads = [
        pltpu.make_async_copy(j_hbm, jb, in_sem.at[0]),
        pltpu.make_async_copy(a_hbm, fld.at[0, :, :, 2:6], in_sem.at[1]),
        pltpu.make_async_copy(g_hbm, gb, in_sem.at[2]),
        pltpu.make_async_copy(w_hbm, wb, in_sem.at[3]),
    ]
    for load in loads:
        load.start()

    sub = lax.broadcasted_iota(jnp.int32, (8, 128), 0)
    lane = lax.broadcasted_iota(jnp.int32, (8, 128), 1)
    sub3 = lax.broadcasted_iota(jnp.int32, (OBJ, 8, 128), 1)

    def put_rows(slot, t, value):
        axs[slot, 0, :, :, t] = value[:, :, 0:1, :]
        axs[slot, 1, :, :, t] = value[:, :, 7:8, :]

    def halo_copies(slot):
        moves = (
            (fld.at[slot, :, :, 2:4], fld.at[slot, :, :, 6:8]),
            (fld.at[slot, :, :, 4:6], fld.at[slot, :, :, 0:2]),
            (axs.at[slot, 0], axh.at[slot, 1]),
            (axs.at[slot, 1], axh.at[slot, 0]),
        )
        return [
            pltpu.make_async_remote_copy(
                src_ref=src, dst_ref=dst, send_sem=send_sem.at[slot, i], recv_sem=recv_sem.at[slot, i],
                device_id=around[i], device_id_type=MESH)
            for i, (src, dst) in enumerate(moves)
        ]

    def local(slot, t):
        if slot == 0:
            acc = -gb[:, :, t]
        else:
            acc = jnp.zeros((OBJ, COMP, 8, 128), F32)
        for o in range(5):
            if 0 <= t + SHIFT[o] < NT:
                for m in range(COMP):
                    near = fld[slot, :, m, 2 + t + SHIFT[o]]
                    acc = acc + jf[o, m, :, t][None] * near[:, None]
        fld[slot + 1, :, :, 2 + t] = acc

    def rest(slot, t):
        acc = fld[slot + 1, :, :, 2 + t]
        for o in range(5):
            if not 0 <= t + SHIFT[o] < NT:
                for m in range(COMP):
                    near = fld[slot, :, m, 2 + t + SHIFT[o]]
                    acc = acc + jf[o, m, :, t][None] * near[:, None]
        for m in range(COMP):
            here = fld[slot, :, m, 2 + t]
            low, high = axh[slot, 0, :, m, t], axh[slot, 1, :, m, t]
            low = jnp.where(ax == 0, F32(0.0), low)
            high = jnp.where(ax == n_ax - 1, F32(0.0), high)
            below = jnp.where(sub3 == 0, low, pltpu.roll(here, 1, 1))
            above = jnp.where(sub3 == 7, high, pltpu.roll(here, 7, 1))
            acc = acc + jf[5, m, :, t][None] * below[:, None]
            acc = acc + jf[6, m, :, t][None] * above[:, None]
        acc = jnp.where(wb[t] == 1, F32(0.0), acc)
        fld[slot + 1, :, :, 2 + t] = acc
        if slot + 1 < SWEEPS:
            put_rows(slot + 1, t, acc)

    def products(wanted):
        names = sorted({s for pair in wanted for s in pair})

        def body(n, sums):
            sums = list(sums)
            for t in range(NT):
                values = {s: fld[s, :, n, 2 + t] for s in names}
                halves = {s: split(values[s]) for s in names}
                for i, (a, b) in enumerate(wanted):
                    p, e = two_prod(values[a], halves[a], values[b], halves[b])
                    s, d = two_sum(sums[i][0], p)
                    sums[i] = (s, sums[i][1] + (d + e))
            return tuple(sums)

        zero = jnp.zeros((OBJ, 8, 128), F32)
        sums = lax.fori_loop(0, COMP, body, ((zero, zero),) * len(wanted))
        parts = [tuple(v[j] for v in s) for s in sums for j in range(OBJ)]
        nothing = jnp.zeros((8, 128), F32)
        return fold_lanes(fold_rows(parts + [(nothing, nothing)] * (8 - len(parts)), sub))

    def on_lanes(part, start):
        return (jnp.where(lane == sub + start, part[0], F32(0.0))
                + jnp.where(lane == sub + (start + 8), part[1], F32(0.0)))

    loads[1].wait()
    for t in range(NT):
        put_rows(0, t, fld[0, :, :, 2 + t])
    loads[0].wait()

    def widen(i, carry):
        for m in range(COMP):
            jf[i, m] = jb[i, m].astype(F32)
        return carry

    lax.fori_loop(0, 7, widen, 0)
    loads[2].wait()
    loads[3].wait()
    pl.semaphore_wait(barrier, len(greeted))

    moving = []
    for slot in range(SWEEPS):
        copies = halo_copies(slot)
        for copy in copies:
            copy.start()
        moving += copies
        for t in range(NT):
            local(slot, t)
        if slot == 2:
            early[...] = on_lanes(products([(1, 1), (1, 2), (2, 2)]), 16)
        for copy in copies:
            copy.wait_recv()
        for t in range(NT):
            rest(slot, t)

    row = on_lanes(products([(1, 3), (2, 3), (3, 3)]), 0) + early[...]
    for k in (4, 2, 1):
        row = row + roll(row, k, 0)
    is_value = (lane // 8) % 2 == 0
    for i, (level, got) in enumerate(zip(levels, (got0, got1, got2))):
        msg[i] = row[0:1]
        for k, offset in enumerate(level):
            pltpu.make_async_remote_copy(
                src_ref=msg.at[i], dst_ref=got.at[k], send_sem=ar_send.at[i], recv_sem=ar_recv.at[i],
                device_id=peer(n_theta, n_ax, **offset), device_id_type=MESH).start()
        pltpu.make_async_copy(got, got, ar_recv.at[i]).wait()
        sums = [(row[0:1], jnp.zeros((1, 128), F32))]
        sums += [(got[k], jnp.zeros((1, 128), F32)) for k in range(len(level))]
        while len(sums) > 1:
            paired = [pair_add(a, b) for a, b in zip(sums[0::2], sums[1::2])]
            sums = paired + sums[2 * len(paired):]
        value, error = (jnp.broadcast_to(v, (8, 128)) for v in sums[0])
        value, error = fast_two_sum(value, error + roll(value, -8, 1) + roll(error, -8, 1))
        row = jnp.where(is_value, value, roll(error, 8, 1))

    def gram(start, k):
        place = start + OBJ * k
        return roll(row, -place, 1), roll(row, -place - 8, 1)

    g02, g12, g22 = (gram(0, k) for k in range(3))
    g00, g01, g11 = (gram(16, k) for k in range(3))
    cells = F32(COMP * NT * 8 * 128 * n_theta * n_ax)
    nothing = jnp.zeros((8, 128), F32)

    def step_of(square):
        mean = jnp.maximum(square[0] + square[1], F32(0.0)) / cells
        return F32(STEP) / jnp.sqrt(mean + F32(EPS))

    c0 = step_of(g00)
    p0 = (c0, nothing)
    square1 = pair_add(g00, pair_mul(p0, pair_add(pair_mul(p0, g11), scaled(g01, -2.0))))
    c1 = step_of(square1)
    both = two_sum(c0, c1)
    times = two_prod(c0, split(c0), c1, split(c1))
    inner = pair_add(pair_mul(both, g11), scaled(g01, -2.0))
    outer = pair_add(scaled(pair_add(g02, scaled(pair_mul(both, g12), -1.0)), 2.0), pair_mul(times, g22))
    square2 = pair_add(g00, pair_add(pair_mul(both, inner), pair_mul(times, outer)))
    c2 = step_of(square2)

    def spread(c):
        picked = [jnp.sum(jnp.where(lane == j, c, F32(0.0)), axis=1, keepdims=True) for j in range(OBJ)]
        return jnp.stack([jnp.broadcast_to(v, (8, 128)) for v in picked])[:, None]

    c0, c1, c2 = spread(c0), spread(c1), spread(c2)
    for t in range(NT):
        f0, f1, f2 = (fld[s, :, :, 2 + t] for s in (1, 2, 3))
        r1 = f0 - c0 * f1
        r2 = r1 - c1 * (f1 - c0 * f2)
        out_ref[:, :, t] = c0 * f0 + c1 * r1 + c2 * r2

    for copy in moving:
        copy.wait_send()
    for i, got in enumerate((got0, got1, got2)):
        pltpu.make_async_copy(got, got, ar_send.at[i]).wait()


def per_device(n_theta, n_ax, adjoint_start, jacobian, objective_gradient, wall_mask):
    field = adjoint_start.shape
    levels = stages(n_theta, n_ax)
    update = pl.pallas_call(
        functools.partial(kernel, n_theta, n_ax),
        out_shape=jax.ShapeDtypeStruct(field, F32),
        in_specs=[pl.BlockSpec(memory_space=pl.ANY)] * 4,
        out_specs=pl.BlockSpec(memory_space=pltpu.VMEM),
        scratch_shapes=[
            pltpu.VMEM((SWEEPS + 1, OBJ, COMP, NT + 4, 8, 128), F32),
            pltpu.VMEM((SWEEPS, 2, OBJ, COMP, NT, 1, 128), F32),
            pltpu.VMEM((SWEEPS, 2, OBJ, COMP, NT, 1, 128), F32),
            pltpu.VMEM(jacobian.shape, jnp.bfloat16),
            pltpu.VMEM(jacobian.shape, F32),
            pltpu.VMEM(field, F32),
            pltpu.VMEM(wall_mask.shape, jnp.int32),
            pltpu.VMEM((8, 128), F32),
            pltpu.VMEM((3, 1, 128), F32),
        ]
        + [pltpu.VMEM((len(level), 1, 128), F32) for level in levels]
        + [
            pltpu.SemaphoreType.DMA((4,)),
            pltpu.SemaphoreType.DMA((SWEEPS, 4)),
            pltpu.SemaphoreType.DMA((SWEEPS, 4)),
            pltpu.SemaphoreType.DMA((3,)),
            pltpu.SemaphoreType.DMA((3,)),
        ],
        compiler_params=pltpu.CompilerParams(collective_id=0, has_side_effects=True),
        name="sweeps",
    )(adjoint_start, jacobian, objective_gradient, wall_mask)
    return adjoint_start - update


def solution(mesh):
    placed = (
        P(None, None, "theta", "ax", None),
        P(None, None, None, "theta", "ax", None),
        P(None, None, "theta", "ax", None),
        P("theta", "ax", None),
    )
    return jax.shard_map(
        functools.partial(per_device, mesh.shape["theta"], mesh.shape["ax"]),
        mesh=mesh,
        in_specs=placed,
        out_specs=P(None, None, "theta", "ax", None),
        check_vma=False,
    )
```

time: 186 us -> 59.3 us (0.32)
  starting transfers between devices: 98.4 us -> 0 us
  Pallas kernels: 0 us -> 56.7 us
  blocking collectives: 42.1 us -> 0 us
  waiting for transfers between devices: 24.6 us -> 0 us
  local copies, waits for them, and re-layouts: 8.61 us -> 0.01 us
  other arithmetic: 10.2 us -> 1.61 us
    pallas_call x0 -> x1, Pallas kernels: none -> 56.7 us  [per_device(): pl.pallas_call(functools.partial(kernel, n_theta, n_ax), out_shape=jax.Sh...]
    ppermute x12 -> x0, starting transfers between devices: 53.2 us -> none  [the longest x6 35.5 us: with_halo(): lax.ppermute(leading, axis, [(b, a) for a, b in up])]
    all_to_all x4 -> x0, starting transfers between devices: 45.1 us -> none  [copy_for_each(): lax.all_to_all(jnp.broadcast_to(value[None], (length, *value.shape)), axi...]
    all_to_all x2 -> x0, blocking collectives: 42.1 us -> none  [copy_for_each(): lax.all_to_all(jnp.broadcast_to(value[None], (length, *value.shape)), axi...]
    all_to_all x4 -> x0, waiting for transfers between devices: 18.7 us -> none  [copy_for_each(): lax.all_to_all(jnp.broadcast_to(value[None], (length, *value.shape)), axi...]
    ppermute x12 -> x0, waiting for transfers between devices: 5.94 us -> none  [the longest x6 5.21 us: with_halo(): lax.ppermute(last, axis, up)]
    slice x6 -> x0, local copies, waits for them, and re-layouts: 3.96 us -> none  [with_halo(): last = lax.slice_in_dim(value, length - width, length, axis=dim)]
    select_n x3 -> x0, other arithmetic: 3.31 us -> none  [exchange_rims(): padded = jnp.where(outside, jnp.float32(0.0), padded)]
  transfers between devices with their start and end apart: 16 -> 0, of which waited for: 5 -> 0; matrix products, arithmetic and copies ran while one was open for 4% -> 0% of each run, Pallas kernels for 0% -> 0%
where the time goes in v1:
time: 59.3 us; the launch traced here: 58.3 us
  Pallas kernels  56.7 us (96%)
  other arithmetic  1.61 us (3%)
    pallas_call x1, Pallas kernels, per_device(): pl.pallas_call(functools.partial(kernel, n_theta, n_ax), out_shape=jax.Sh...  56.7 us
    sub x1, other arithmetic, per_device(): return adjoint_start - update  1.61 us

profile of v1, /device:TPU:1, one launch (start us, length us, event | category | flops | bytes accessed | tf_op | source)
XLA Modules:
  0.0 58.3 jit_solution(8696917082408749333)
XLA Ops:
  0.0 0.0 copy-start
  0.0 56.7 %sweeps.1 = f32[2,5,4,8,128]{4,3,2,1,0:T(8,128)} custom-call(f32[2,5,4,8,128]{4,3,2,1,0:T(8,128)} %a_hbm.1, bf16[7,5,5,4,8,128]{5,4,3,2,1,0:T(8,128)(2,1)} %j_hbm.1, f32[2,5,4,8,128]{4,3,2,1,0:T(8,128)} %g_hbm.1, s32[4,8,128]{2,1,0:T(8,128)} %w_hbm.1), custom_call_target="tpu_custom_call" | custom-call | tf_op jit(solution)/shard_map/sweeps/pallas_call | solution.py:319
  56.7 0.0 copy-done
  56.7 1.6 %sub.3 = f32[2,5,4,8,128]{4,3,2,1,0:T(8,128)} subtract(f32[2,5,4,8,128]{4,3,2,1,0:T(8,128)S(1)} %copy-done, f32[2,5,4,8,128]{4,3,2,1,0:T(8,128)} %sweeps.1) | non-fusion elementwise | flops 40960 | bytes 491520 | tf_op jit(solution)/shard_map/sub | solution.py:346
Async XLA Ops:
  0.0 56.7 %copy-start = (f32[2,5,4,8,128]{4,3,2,1,0:T(8,128)S(1)}, f32[2,5,4,8,128]{4,3,2,1,0:T(8,128)}, u32[]{:S(2)}) copy-start(f32[2,5,4,8,128]{4,3,2,1,0:T(8,128)} %a_hbm.1) | copy-start | bytes 491524

commit v2 on v1

--- a/solution.py
+++ b/solution.py
@@ -45,13 +45,17 @@
 
 def stages(n_theta, n_ax):
     nz, ny = n_theta // (YL * CORES), (n_ax // X) * YL
-    pairs = [(dx, dc) for dx in range(X) for dc in range(CORES) if dx or dc]
-    pairs.sort(key=lambda p: (-min(p[0], X - p[0]), p[1]))
+    plane = [(dx, dy) for dx in range(X) for dy in range(ny) if dx or dy]
+    plane.sort(key=lambda p: -min(p[0], X - p[0]) - min(p[1], ny - p[1]))
+    ring = [(dz, dc) for dz in near_last(nz) + [0] for dc in range(CORES) if dz or dc]
     return (
-        [dict(dx=dx, dc=dc) for dx, dc in pairs],
-        [dict(dy=dy) for dy in near_last(ny)],
-        [dict(dz=dz) for dz in near_last(nz)],
+        [dict(dx=dx, dy=dy) for dx, dy in plane],
+        [dict(dz=dz, dc=dc) for dz, dc in ring],
     )
+
+
+def rows_of(level):
+    return -(-(len(level) + 1) // 8) * 8
 
 
 def two_sum(a, b):
@@ -119,8 +123,8 @@
 
 
 def kernel(n_theta, n_ax, a_hbm, j_hbm, g_hbm, w_hbm, out_ref,
-           fld, axs, axh, jb, jf, gb, wb, early, msg, got0, got1, got2,
-           in_sem, send_sem, recv_sem, ar_send, ar_recv):
+           fld, axh, jb, jf, je, gb, wb, early, msg, got0, got1,
+           in_sem, send_sem, recv_sem, ar_send, ar_recv, ready):
     theta, ax = lax.axis_index("theta"), lax.axis_index("ax")
     around = [
         ((theta + n_theta - 1) % n_theta, ax),
@@ -130,9 +134,28 @@
     ]
     levels = stages(n_theta, n_ax)
     barrier = pltpu.get_barrier_semaphore()
-    greeted = around + [peer(n_theta, n_ax, **p) for level in reversed(levels) for p in level]
-    for dev in greeted:
-        pl.semaphore_signal(barrier, inc=1, device_id=dev, device_id_type=MESH)
+    nz, ny = n_theta // (YL * CORES), (n_ax // X) * YL
+
+    def tell(sem, devices):
+        for dev in devices:
+            pl.semaphore_signal(sem, inc=1, device_id=dev, device_id_type=MESH)
+
+    near = (-3, -2, -1, 1, 2, 3)
+    offsets = (
+        [dict(dc=1)]
+        + [dict(dx=d) for d in range(1, X)]
+        + [dict(dy=d) for d in sorted({k % ny for k in near} - {0})]
+        + [dict(dz=d) for d in sorted({k % nz for k in near} - {0})]
+    )
+    two, three = min(2, nz - 1), min(3, nz - 1)
+    columns = [dict(dx=d) for d in range(1, X)]
+    first = columns + [dict(dc=1), dict(dy=ny - 1), dict(dz=three), dict(dz=nz - three)]
+    second = columns + [dict(dz=two), dict(dz=nz - two), dict(dz=three, dc=1), dict(dz=nz - three, dc=1)]
+    greeted = around + [peer(n_theta, n_ax, **p) for p in offsets]
+    tell(barrier, around)
+    for level, got in zip(levels, (got0, got1)):
+        if len(level) + 1 < got.shape[0]:
+            got[len(level) + 1 :] = jnp.zeros((got.shape[0] - len(level) - 1, 128), F32)
 
     loads = [
         pltpu.make_async_copy(j_hbm, jb, in_sem.at[0]),
@@ -142,21 +165,20 @@
     ]
     for load in loads:
         load.start()
+    tell(barrier, greeted[len(around):])
+    pl.semaphore_wait(barrier, len(greeted))
 
     sub = lax.broadcasted_iota(jnp.int32, (8, 128), 0)
     lane = lax.broadcasted_iota(jnp.int32, (8, 128), 1)
     sub3 = lax.broadcasted_iota(jnp.int32, (OBJ, 8, 128), 1)
 
-    def put_rows(slot, t, value):
-        axs[slot, 0, :, :, t] = value[:, :, 0:1, :]
-        axs[slot, 1, :, :, t] = value[:, :, 7:8, :]
-
     def halo_copies(slot):
+        mine = a_hbm if slot == 0 else fld.at[slot, :, :, 2:6]
         moves = (
-            (fld.at[slot, :, :, 2:4], fld.at[slot, :, :, 6:8]),
-            (fld.at[slot, :, :, 4:6], fld.at[slot, :, :, 0:2]),
-            (axs.at[slot, 0], axh.at[slot, 1]),
-            (axs.at[slot, 1], axh.at[slot, 0]),
+            (mine.at[:, :, 0:2], fld.at[slot, :, :, 6:8]),
+            (mine.at[:, :, 2:4], fld.at[slot, :, :, 0:2]),
+            (mine.at[:, :, :, 0:1], axh.at[slot, 1]),
+            (mine.at[:, :, :, 7:8], axh.at[slot, 0]),
         )
         return [
             pltpu.make_async_remote_copy(
@@ -165,110 +187,125 @@
             for i, (src, dst) in enumerate(moves)
         ]
 
-    def local(slot, t):
-        if slot == 0:
-            acc = -gb[:, :, t]
-        else:
-            acc = jnp.zeros((OBJ, COMP, 8, 128), F32)
+    def theta_part(acc, slot, t, inside):
         for o in range(5):
-            if 0 <= t + SHIFT[o] < NT:
+            if (0 <= t + SHIFT[o] < NT) == inside:
                 for m in range(COMP):
                     near = fld[slot, :, m, 2 + t + SHIFT[o]]
                     acc = acc + jf[o, m, :, t][None] * near[:, None]
-        fld[slot + 1, :, :, 2 + t] = acc
-
-    def rest(slot, t):
-        acc = fld[slot + 1, :, :, 2 + t]
-        for o in range(5):
-            if not 0 <= t + SHIFT[o] < NT:
-                for m in range(COMP):
-                    near = fld[slot, :, m, 2 + t + SHIFT[o]]
-                    acc = acc + jf[o, m, :, t][None] * near[:, None]
+        return acc
+
+    def local(slot, t):
+        acc = -gb[:, :, t] if slot == 0 else jnp.zeros((OBJ, COMP, 8, 128), F32)
+        acc = theta_part(acc, slot, t, True)
         for m in range(COMP):
             here = fld[slot, :, m, 2 + t]
-            low, high = axh[slot, 0, :, m, t], axh[slot, 1, :, m, t]
-            low = jnp.where(ax == 0, F32(0.0), low)
-            high = jnp.where(ax == n_ax - 1, F32(0.0), high)
-            below = jnp.where(sub3 == 0, low, pltpu.roll(here, 1, 1))
-            above = jnp.where(sub3 == 7, high, pltpu.roll(here, 7, 1))
+            below = jnp.where(sub3 == 0, F32(0.0), pltpu.roll(here, 1, 1))
+            above = jnp.where(sub3 == 7, F32(0.0), pltpu.roll(here, 7, 1))
             acc = acc + jf[5, m, :, t][None] * below[:, None]
             acc = acc + jf[6, m, :, t][None] * above[:, None]
+        fld[slot + 1, :, :, 2 + t] = acc
+
+    def rest(slot, t):
+        acc = theta_part(fld[slot + 1, :, :, 2 + t], slot, t, False)
+        for m in range(COMP):
+            edge = jnp.where(sub3 < 4, axh[slot, 0, :, m, t], axh[slot, 1, :, m, t])
+            acc = acc + je[m, :, t][None] * edge[:, None]
         acc = jnp.where(wb[t] == 1, F32(0.0), acc)
         fld[slot + 1, :, :, 2 + t] = acc
-        if slot + 1 < SWEEPS:
-            put_rows(slot + 1, t, acc)
-
-    def products(wanted):
-        names = sorted({s for pair in wanted for s in pair})
-
-        def body(n, sums):
-            sums = list(sums)
-            for t in range(NT):
-                values = {s: fld[s, :, n, 2 + t] for s in names}
-                halves = {s: split(values[s]) for s in names}
-                for i, (a, b) in enumerate(wanted):
-                    p, e = two_prod(values[a], halves[a], values[b], halves[b])
-                    s, d = two_sum(sums[i][0], p)
-                    sums[i] = (s, sums[i][1] + (d + e))
-            return tuple(sums)
-
-        zero = jnp.zeros((OBJ, 8, 128), F32)
-        sums = lax.fori_loop(0, COMP, body, ((zero, zero),) * len(wanted))
+        return acc
+
+    def add_products(sums, values, wanted):
+        halves = {s: split(v) for s, v in values.items()}
+        sums = list(sums)
+        for i, (a, b) in enumerate(wanted):
+            p, e = two_prod(values[a], halves[a], values[b], halves[b])
+            s, d = two_sum(sums[i][0], p)
+            sums[i] = (s, sums[i][1] + (d + e))
+        return sums
+
+    zero = jnp.zeros((OBJ, 8, 128), F32)
+
+    def folded(sums):
         parts = [tuple(v[j] for v in s) for s in sums for j in range(OBJ)]
         nothing = jnp.zeros((8, 128), F32)
         return fold_lanes(fold_rows(parts + [(nothing, nothing)] * (8 - len(parts)), sub))
 
+    def early_products(n, sums):
+        for t in range(NT):
+            values = {s: fld[s, :, n, 2 + t] for s in (1, 2)}
+            sums = add_products(sums, values, ((1, 1), (1, 2), (2, 2)))
+        return tuple(sums)
+
     def on_lanes(part, start):
         return (jnp.where(lane == sub + start, part[0], F32(0.0))
                 + jnp.where(lane == sub + (start + 8), part[1], F32(0.0)))
 
-    loads[1].wait()
-    for t in range(NT):
-        put_rows(0, t, fld[0, :, :, 2 + t])
-    loads[0].wait()
-
-    def widen(i, carry):
-        for m in range(COMP):
-            jf[i, m] = jb[i, m].astype(F32)
-        return carry
-
-    lax.fori_loop(0, 7, widen, 0)
-    loads[2].wait()
-    loads[3].wait()
-    pl.semaphore_wait(barrier, len(greeted))
-
     moving = []
     for slot in range(SWEEPS):
         copies = halo_copies(slot)
-        for copy in copies:
+        for copy in (copies[2], copies[3], copies[0], copies[1]):
             copy.start()
         moving += copies
+        if slot == 0:
+            tell(ready.at[0], [peer(n_theta, n_ax, **p) for p in first])
+            loads[0].wait()
+
+            def widen(i, carry):
+                for m in range(COMP):
+                    jf[i, m] = jb[i, m].astype(F32)
+                return carry
+
+            lax.fori_loop(0, 7, widen, 0)
+            low = jnp.where(sub == 0, jnp.where(ax == 0, F32(0.0), F32(1.0)), F32(0.0))
+            high = jnp.where(sub == 7, jnp.where(ax == n_ax - 1, F32(0.0), F32(1.0)), F32(0.0))
+
+            def edges(m, carry):
+                je[m] = jf[5, m] * low + jf[6, m] * high
+                return carry
+
+            lax.fori_loop(0, COMP, edges, 0)
+            for load in loads[1:]:
+                load.wait()
         for t in range(NT):
             local(slot, t)
         if slot == 2:
-            early[...] = on_lanes(products([(1, 1), (1, 2), (2, 2)]), 16)
+            early[...] = on_lanes(folded(lax.fori_loop(0, COMP, early_products, ((zero, zero),) * 3)), 16)
         for copy in copies:
             copy.wait_recv()
+        if slot == 1:
+            pl.semaphore_wait(ready.at[0], len(first))
+            tell(ready.at[1], [peer(n_theta, n_ax, **p) for p in second])
+        if slot == 2:
+            pl.semaphore_wait(ready.at[1], len(second))
+        sums = [(zero, zero)] * 3
         for t in range(NT):
-            rest(slot, t)
-
-    row = on_lanes(products([(1, 3), (2, 3), (3, 3)]), 0) + early[...]
+            acc = rest(slot, t)
+            if slot == 2:
+                for n in range(COMP):
+                    values = {1: fld[1, :, n, 2 + t], 2: fld[2, :, n, 2 + t], 3: acc[:, n]}
+                    sums = add_products(sums, values, ((1, 3), (2, 3), (3, 3)))
+
+    row = on_lanes(folded(sums), 0) + early[...]
     for k in (4, 2, 1):
         row = row + roll(row, k, 0)
     is_value = (lane // 8) % 2 == 0
-    for i, (level, got) in enumerate(zip(levels, (got0, got1, got2))):
-        msg[i] = row[0:1]
+    for i, (level, got) in enumerate(zip(levels, (got0, got1))):
+        msg[i] = row
         for k, offset in enumerate(level):
             pltpu.make_async_remote_copy(
-                src_ref=msg.at[i], dst_ref=got.at[k], send_sem=ar_send.at[i], recv_sem=ar_recv.at[i],
-                device_id=peer(n_theta, n_ax, **offset), device_id_type=MESH).start()
-        pltpu.make_async_copy(got, got, ar_recv.at[i]).wait()
-        sums = [(row[0:1], jnp.zeros((1, 128), F32))]
-        sums += [(got[k], jnp.zeros((1, 128), F32)) for k in range(len(level))]
+                src_ref=msg.at[i, 0:1], dst_ref=got.at[k : k + 1], send_sem=ar_send.at[i],
+                recv_sem=ar_recv.at[i], device_id=peer(n_theta, n_ax, **offset), device_id_type=MESH).start()
+        got[len(level) : len(level) + 1] = row[0:1]
+        heard = got.at[0 : len(level)]
+        pltpu.make_async_copy(heard, heard, ar_recv.at[i]).wait()
+        sums = [(got[k : k + 8], jnp.zeros((8, 128), F32)) for k in range(0, got.shape[0], 8)]
         while len(sums) > 1:
             paired = [pair_add(a, b) for a, b in zip(sums[0::2], sums[1::2])]
             sums = paired + sums[2 * len(paired):]
-        value, error = (jnp.broadcast_to(v, (8, 128)) for v in sums[0])
+        value, error = sums[0]
+        for k in (4, 2, 1):
+            value, error = pair_add((value, error), (roll(value, k, 0), roll(error, k, 0)))
         value, error = fast_two_sum(value, error + roll(value, -8, 1) + roll(error, -8, 1))
         row = jnp.where(is_value, value, roll(error, 8, 1))
 
@@ -309,8 +346,9 @@
 
     for copy in moving:
         copy.wait_send()
-    for i, got in enumerate((got0, got1, got2)):
-        pltpu.make_async_copy(got, got, ar_send.at[i]).wait()
+    for i, got in enumerate((got0, got1)):
+        heard = got.at[0 : len(levels[i])]
+        pltpu.make_async_copy(heard, heard, ar_send.at[i]).wait()
 
 
 def per_device(n_theta, n_ax, adjoint_start, jacobian, objective_gradient, wall_mask):
@@ -318,27 +356,28 @@
     levels = stages(n_theta, n_ax)
     update = pl.pallas_call(
         functools.partial(kernel, n_theta, n_ax),
-        out_shape=jax.ShapeDtypeStruct(field, F32),
+        out_shape=pltpu.VMEM(field, F32),
         in_specs=[pl.BlockSpec(memory_space=pl.ANY)] * 4,
         out_specs=pl.BlockSpec(memory_space=pltpu.VMEM),
         scratch_shapes=[
             pltpu.VMEM((SWEEPS + 1, OBJ, COMP, NT + 4, 8, 128), F32),
             pltpu.VMEM((SWEEPS, 2, OBJ, COMP, NT, 1, 128), F32),
-            pltpu.VMEM((SWEEPS, 2, OBJ, COMP, NT, 1, 128), F32),
             pltpu.VMEM(jacobian.shape, jnp.bfloat16),
             pltpu.VMEM(jacobian.shape, F32),
+            pltpu.VMEM((COMP, COMP, NT, 8, 128), F32),
             pltpu.VMEM(field, F32),
             pltpu.VMEM(wall_mask.shape, jnp.int32),
             pltpu.VMEM((8, 128), F32),
-            pltpu.VMEM((3, 1, 128), F32),
+            pltpu.VMEM((2, 8, 128), F32),
         ]
-        + [pltpu.VMEM((len(level), 1, 128), F32) for level in levels]
+        + [pltpu.VMEM((rows_of(level), 128), F32) for level in levels]
         + [
             pltpu.SemaphoreType.DMA((4,)),
             pltpu.SemaphoreType.DMA((SWEEPS, 4)),
             pltpu.SemaphoreType.DMA((SWEEPS, 4)),
-            pltpu.SemaphoreType.DMA((3,)),
-            pltpu.SemaphoreType.DMA((3,)),
+            pltpu.SemaphoreType.DMA((2,)),
+            pltpu.SemaphoreType.DMA((2,)),
+            pltpu.SemaphoreType.REGULAR((2,)),
         ],
         compiler_params=pltpu.CompilerParams(collective_id=0, has_side_effects=True),
         name="sweeps",

time: 59.3 us -> 51 us (0.86); the launches traced: 58.3 us -> 50.8 us
  Pallas kernels: 56.7 us -> 50.1 us
  other arithmetic: 1.61 us -> 0.69 us
    pallas_call x1, Pallas kernels: 56.7 us -> 50.1 us  [per_device(): pl.pallas_call(functools.partial(kernel, n_theta, n_ax), out_shape=pltpu....]
    sub x1, other arithmetic: 1.61 us -> 0.69 us  [per_device(): return adjoint_start - update]
where the time goes in v2:
time: 51 us; the launch traced here: 50.8 us
  Pallas kernels  50.1 us (98%)
  other arithmetic  0.69 us (1%)
    pallas_call x1, Pallas kernels, per_device(): pl.pallas_call(functools.partial(kernel, n_theta, n_ax), out_shape=pltpu....  50.1 us

profile of v2, /device:TPU:1, one launch (start us, length us, event | category | flops | bytes accessed | tf_op | source)
XLA Modules:
  0.0 50.8 jit_solution(11279024741712242636)
XLA Ops:
  0.0 0.0 copy-start
  0.0 50.1 %sweeps.1 = f32[2,5,4,8,128]{4,3,2,1,0:T(8,128)S(1)} custom-call(f32[2,5,4,8,128]{4,3,2,1,0:T(8,128)} %a_hbm.1, bf16[7,5,5,4,8,128]{5,4,3,2,1,0:T(8,128)(2,1)} %j_hbm.1, f32[2,5,4,8,128]{4,3,2,1,0:T(8,128)} %g_hbm.1, s32[4,8,128]{2,1,0:T(8,128)} %w_hbm.1), custom_call_target="tpu_custom_call" | custom-call | tf_op jit(solution)/shard_map/sweeps/pallas_call | solution.py:357
  50.1 0.0 copy-done
  50.2 0.7 %sub.3 = f32[2,5,4,8,128]{4,3,2,1,0:T(8,128)} subtract(f32[2,5,4,8,128]{4,3,2,1,0:T(8,128)S(1)} %copy-done, f32[2,5,4,8,128]{4,3,2,1,0:T(8,128)S(1)} %sweeps.1) | non-fusion elementwise | flops 40960 | bytes 491520 | tf_op jit(solution)/shard_map/sub | solution.py:385
Async XLA Ops:
  0.0 50.1 %copy-start = (f32[2,5,4,8,128]{4,3,2,1,0:T(8,128)S(1)}, f32[2,5,4,8,128]{4,3,2,1,0:T(8,128)}, u32[]{:S(2)}) copy-start(f32[2,5,4,8,128]{4,3,2,1,0:T(8,128)} %a_hbm.1) | copy-start | bytes 491524

commit v3 on v2

--- a/solution.py
+++ b/solution.py
@@ -124,7 +124,7 @@
 
 def kernel(n_theta, n_ax, a_hbm, j_hbm, g_hbm, w_hbm, out_ref,
            fld, axh, jb, jf, je, gb, wb, early, msg, got0, got1,
-           in_sem, send_sem, recv_sem, ar_send, ar_recv, ready):
+           in_sem, send_sem, recv_sem, ar_recv, ready):
     theta, ax = lax.axis_index("theta"), lax.axis_index("ax")
     around = [
         ((theta + n_theta - 1) % n_theta, ax),
@@ -140,19 +140,30 @@
         for dev in devices:
             pl.semaphore_signal(sem, inc=1, device_id=dev, device_id_type=MESH)
 
-    near = (-3, -2, -1, 1, 2, 3)
-    offsets = (
-        [dict(dc=1)]
-        + [dict(dx=d) for d in range(1, X)]
-        + [dict(dy=d) for d in sorted({k % ny for k in near} - {0})]
-        + [dict(dz=d) for d in sorted({k % nz for k in near} - {0})]
+    rows = [dict(dx=d) for d in range(1, X)]
+
+    def ring(name, size, *distances):
+        return [{name: d} for d in sorted({k % size for k in distances} - {0})]
+
+    offsets = rows + [dict(dc=1)] + ring("dy", ny, 1, -1) + ring("dz", nz, 1, -1)
+    relays = (
+        offsets,
+        rows + [dict(dc=1)] + ring("dy", ny, 2, -2) + ring("dz", nz, 2, -2),
+        rows + ring("dz", nz, 4, -4),
+        [dict(dc=1)],
     )
-    two, three = min(2, nz - 1), min(3, nz - 1)
-    columns = [dict(dx=d) for d in range(1, X)]
-    first = columns + [dict(dc=1), dict(dy=ny - 1), dict(dz=three), dict(dz=nz - three)]
-    second = columns + [dict(dz=two), dict(dz=nz - two), dict(dz=three, dc=1), dict(dz=nz - three, dc=1)]
-    greeted = around + [peer(n_theta, n_ax, **p) for p in offsets]
-    tell(barrier, around)
+
+    def relay(i):
+        if i:
+            pl.semaphore_wait(ready.at[i - 1], len(relays[i - 1]))
+        if i < len(relays):
+            tell(ready.at[i], [peer(n_theta, n_ax, **p) for p in relays[i]])
+
+    has = (1, 1, (ax + n_ax - 1) // n_ax, 1 - (ax + 1) // n_ax)
+    middle = has[2] * has[3]
+    tell(barrier, around[:2])
+    for side in (2, 3):
+        pl.when(has[side] == 1)(functools.partial(tell, barrier, around[side : side + 1]))
     for level, got in zip(levels, (got0, got1)):
         if len(level) + 1 < got.shape[0]:
             got[len(level) + 1 :] = jnp.zeros((got.shape[0] - len(level) - 1, 128), F32)
@@ -160,17 +171,26 @@
     loads = [
         pltpu.make_async_copy(j_hbm, jb, in_sem.at[0]),
         pltpu.make_async_copy(a_hbm, fld.at[0, :, :, 2:6], in_sem.at[1]),
-        pltpu.make_async_copy(g_hbm, gb, in_sem.at[2]),
-        pltpu.make_async_copy(w_hbm, wb, in_sem.at[3]),
+        pltpu.make_async_copy(g_hbm, gb, in_sem.at[1]),
+        pltpu.make_async_copy(w_hbm, wb, in_sem.at[1]),
     ]
     for load in loads:
         load.start()
-    tell(barrier, greeted[len(around):])
-    pl.semaphore_wait(barrier, len(greeted))
+    tell(barrier, [peer(n_theta, n_ax, **p) for p in offsets])
+    for side in (0, 1):
+
+        @pl.when(has[2 + side] == 0)
+        def _():
+            axh[:, side] = jnp.zeros((SWEEPS, OBJ, COMP, NT, 1, 128), F32)
+
+    pl.semaphore_wait(barrier, len(offsets) + 2 + has[2] + has[3])
 
     sub = lax.broadcasted_iota(jnp.int32, (8, 128), 0)
     lane = lax.broadcasted_iota(jnp.int32, (8, 128), 1)
     sub3 = lax.broadcasted_iota(jnp.int32, (OBJ, 8, 128), 1)
+
+    def await_tiles(sem, like):
+        pltpu.make_async_copy(like, like, sem).wait()
 
     def halo_copies(slot):
         mine = a_hbm if slot == 0 else fld.at[slot, :, :, 2:6]
@@ -182,7 +202,7 @@
         )
         return [
             pltpu.make_async_remote_copy(
-                src_ref=src, dst_ref=dst, send_sem=send_sem.at[slot, i], recv_sem=recv_sem.at[slot, i],
+                src_ref=src, dst_ref=dst, send_sem=send_sem.at[0], recv_sem=recv_sem.at[slot, i // 2],
                 device_id=around[i], device_id_type=MESH)
             for i, (src, dst) in enumerate(moves)
         ]
@@ -207,7 +227,7 @@
         fld[slot + 1, :, :, 2 + t] = acc
 
     def rest(slot, t):
-        acc = theta_part(fld[slot + 1, :, :, 2 + t], slot, t, False)
+        acc = fld[slot + 1, :, :, 2 + t]
         for m in range(COMP):
             edge = jnp.where(sub3 < 4, axh[slot, 0, :, m, t], axh[slot, 1, :, m, t])
             acc = acc + je[m, :, t][None] * edge[:, None]
@@ -241,14 +261,14 @@
         return (jnp.where(lane == sub + start, part[0], F32(0.0))
                 + jnp.where(lane == sub + (start + 8), part[1], F32(0.0)))
 
-    moving = []
     for slot in range(SWEEPS):
         copies = halo_copies(slot)
-        for copy in (copies[2], copies[3], copies[0], copies[1]):
-            copy.start()
-        moving += copies
+        for i in (2, 3):
+            pl.when(has[i] == 1)(copies[i].start)
+        for i in (0, 1):
+            copies[i].start()
+        relay(slot)
         if slot == 0:
-            tell(ready.at[0], [peer(n_theta, n_ax, **p) for p in first])
             loads[0].wait()
 
             def widen(i, carry):
@@ -257,8 +277,8 @@
                 return carry
 
             lax.fori_loop(0, 7, widen, 0)
-            low = jnp.where(sub == 0, jnp.where(ax == 0, F32(0.0), F32(1.0)), F32(0.0))
-            high = jnp.where(sub == 7, jnp.where(ax == n_ax - 1, F32(0.0), F32(1.0)), F32(0.0))
+            low = jnp.where(sub == 0, F32(1.0), F32(0.0))
+            high = jnp.where(sub == 7, F32(1.0), F32(0.0))
 
             def edges(m, carry):
                 je[m] = jf[5, m] * low + jf[6, m] * high
@@ -271,13 +291,12 @@
             local(slot, t)
         if slot == 2:
             early[...] = on_lanes(folded(lax.fori_loop(0, COMP, early_products, ((zero, zero),) * 3)), 16)
-        for copy in copies:
-            copy.wait_recv()
-        if slot == 1:
-            pl.semaphore_wait(ready.at[0], len(first))
-            tell(ready.at[1], [peer(n_theta, n_ax, **p) for p in second])
-        if slot == 2:
-            pl.semaphore_wait(ready.at[1], len(second))
+            relay(3)
+        await_tiles(recv_sem.at[slot, 0], je.at[:, 0:4, 0:2])
+        for t in range(NT):
+            fld[slot + 1, :, :, 2 + t] = theta_part(fld[slot + 1, :, :, 2 + t], slot, t, False)
+        pl.when(middle == 1)(functools.partial(await_tiles, recv_sem.at[slot, 1], je.at[:, 0:2, 0:1]))
+        pl.when(middle == 0)(functools.partial(await_tiles, recv_sem.at[slot, 1], je.at[:, 0:1, 0:1]))
         sums = [(zero, zero)] * 3
         for t in range(NT):
             acc = rest(slot, t)
@@ -292,9 +311,11 @@
     is_value = (lane // 8) % 2 == 0
     for i, (level, got) in enumerate(zip(levels, (got0, got1))):
         msg[i] = row
+        if i == 1:
+            relay(4)
         for k, offset in enumerate(level):
             pltpu.make_async_remote_copy(
-                src_ref=msg.at[i, 0:1], dst_ref=got.at[k : k + 1], send_sem=ar_send.at[i],
+                src_ref=msg.at[i, 0:1], dst_ref=got.at[k : k + 1], send_sem=send_sem.at[1],
                 recv_sem=ar_recv.at[i], device_id=peer(n_theta, n_ax, **offset), device_id_type=MESH).start()
         got[len(level) : len(level) + 1] = row[0:1]
         heard = got.at[0 : len(level)]
@@ -344,11 +365,11 @@
         r2 = r1 - c1 * (f1 - c0 * f2)
         out_ref[:, :, t] = c0 * f0 + c1 * r1 + c2 * r2
 
-    for copy in moving:
-        copy.wait_send()
-    for i, got in enumerate((got0, got1)):
-        heard = got.at[0 : len(levels[i])]
-        pltpu.make_async_copy(heard, heard, ar_send.at[i]).wait()
+    pl.when(middle == 1)(functools.partial(await_tiles, send_sem.at[0], jf.at[0:6, :, :, 0:1]))
+    pl.when(middle == 0)(functools.partial(await_tiles, send_sem.at[0], jf.at[0:3, 0:3, :, 0:3]))
+    for i in range(2):
+        heard = (got0, got1)[i].at[0 : len(levels[i])]
+        pltpu.make_async_copy(heard, heard, send_sem.at[1]).wait()
 
 
 def per_device(n_theta, n_ax, adjoint_start, jacobian, objective_gradient, wall_mask):
@@ -372,12 +393,11 @@
         ]
         + [pltpu.VMEM((rows_of(level), 128), F32) for level in levels]
         + [
-            pltpu.SemaphoreType.DMA((4,)),
-            pltpu.SemaphoreType.DMA((SWEEPS, 4)),
-            pltpu.SemaphoreType.DMA((SWEEPS, 4)),
             pltpu.SemaphoreType.DMA((2,)),
             pltpu.SemaphoreType.DMA((2,)),
-            pltpu.SemaphoreType.REGULAR((2,)),
+            pltpu.SemaphoreType.DMA((SWEEPS, 2)),
+            pltpu.SemaphoreType.DMA((2,)),
+            pltpu.SemaphoreType.REGULAR((4,)),
         ],
         compiler_params=pltpu.CompilerParams(collective_id=0, has_side_effects=True),
         name="sweeps",

time: 51 us -> 49.8 us (0.976)
  Pallas kernels: 50.1 us -> 49 us
    pallas_call x1, Pallas kernels: 50.1 us -> 49 us  [per_device(): pl.pallas_call(functools.partial(kernel, n_theta, n_ax), out_shape=pltpu....]
where the time goes in v3:
time: 49.8 us; the launch traced here: 49.7 us
  Pallas kernels  49 us (98%)
  other arithmetic  0.69 us (1%)
    pallas_call x1, Pallas kernels, per_device(): pl.pallas_call(functools.partial(kernel, n_theta, n_ax), out_shape=pltpu....  49 us

profile of v3, /device:TPU:1, one launch (start us, length us, event | category | flops | bytes accessed | tf_op | source)
XLA Modules:
  0.0 49.7 jit_solution(6173433610172717477)
XLA Ops:
  0.0 0.0 copy-start
  0.0 49.0 %sweeps.1 = f32[2,5,4,8,128]{4,3,2,1,0:T(8,128)S(1)} custom-call(f32[2,5,4,8,128]{4,3,2,1,0:T(8,128)} %a_hbm.1, bf16[7,5,5,4,8,128]{5,4,3,2,1,0:T(8,128)(2,1)} %j_hbm.1, f32[2,5,4,8,128]{4,3,2,1,0:T(8,128)} %g_hbm.1, s32[4,8,128]{2,1,0:T(8,128)} %w_hbm.1), custom_call_target="tpu_custom_call" | custom-call | tf_op jit(solution)/shard_map/sweeps/pallas_call | solution.py:378
  49.0 0.0 copy-done
  49.0 0.7 %sub.3 = f32[2,5,4,8,128]{4,3,2,1,0:T(8,128)} subtract(f32[2,5,4,8,128]{4,3,2,1,0:T(8,128)S(1)} %copy-done, f32[2,5,4,8,128]{4,3,2,1,0:T(8,128)S(1)} %sweeps.1) | non-fusion elementwise | flops 40960 | bytes 491520 | tf_op jit(solution)/shard_map/sub | solution.py:405
Async XLA Ops:
  0.0 49.0 %copy-start = (f32[2,5,4,8,128]{4,3,2,1,0:T(8,128)S(1)}, f32[2,5,4,8,128]{4,3,2,1,0:T(8,128)}, u32[]{:S(2)}) copy-start(f32[2,5,4,8,128]{4,3,2,1,0:T(8,128)} %a_hbm.1) | copy-start | bytes 491524

commit v4 on v3

--- a/solution.py
+++ b/solution.py
@@ -116,10 +116,19 @@
     return parts[0]
 
 
+def rolled(part, shift, axis):
+    return tuple(roll(v, shift, axis) for v in part)
+
+
+def fold_four(part, k, axis):
+    near = pair_add(part, rolled(part, k, axis))
+    return pair_add(near, pair_add(rolled(part, 2 * k, axis), rolled(part, 3 * k, axis)))
+
+
 def fold_lanes(part):
-    for k in (64, 32, 16, 8, 4, 2, 1):
-        part = pair_add(part, tuple(roll(v, k, 1) for v in part))
-    return norm_pair(part)
+    for k in (32, 8, 2):
+        part = fold_four(part, k, 1)
+    return norm_pair(pair_add(part, rolled(part, 1, 1)))
 
 
 def kernel(n_theta, n_ax, a_hbm, j_hbm, g_hbm, w_hbm, out_ref,
@@ -325,8 +334,8 @@
             paired = [pair_add(a, b) for a, b in zip(sums[0::2], sums[1::2])]
             sums = paired + sums[2 * len(paired):]
         value, error = sums[0]
-        for k in (4, 2, 1):
-            value, error = pair_add((value, error), (roll(value, k, 0), roll(error, k, 0)))
+        value, error = fold_four((value, error), 2, 0)
+        value, error = pair_add((value, error), (roll(value, 1, 0), roll(error, 1, 0)))
         value, error = fast_two_sum(value, error + roll(value, -8, 1) + roll(error, -8, 1))
         row = jnp.where(is_value, value, roll(error, 8, 1))
 

time: 49.8 us -> 49.6 us (level)
  no operation moved by 1% of the time
where the time goes in v4:
time: 49.6 us; the launch traced here: 49.5 us
  Pallas kernels  48.8 us (98%)
  other arithmetic  0.69 us (1%)
    pallas_call x1, Pallas kernels, per_device(): pl.pallas_call(functools.partial(kernel, n_theta, n_ax), out_shape=pltpu....  48.8 us

profile of v4, /device:TPU:1, one launch (start us, length us, event | category | flops | bytes accessed | tf_op | source)
XLA Modules:
  0.0 49.5 jit_solution(12229983831311317060)
XLA Ops:
  0.0 0.0 copy-start
  0.0 48.8 %sweeps.1 = f32[2,5,4,8,128]{4,3,2,1,0:T(8,128)S(1)} custom-call(f32[2,5,4,8,128]{4,3,2,1,0:T(8,128)} %a_hbm.1, bf16[7,5,5,4,8,128]{5,4,3,2,1,0:T(8,128)(2,1)} %j_hbm.1, f32[2,5,4,8,128]{4,3,2,1,0:T(8,128)} %g_hbm.1, s32[4,8,128]{2,1,0:T(8,128)} %w_hbm.1), custom_call_target="tpu_custom_call" | custom-call | tf_op jit(solution)/shard_map/sweeps/pallas_call | solution.py:387
  48.8 0.0 copy-done
  48.8 0.7 %sub.3 = f32[2,5,4,8,128]{4,3,2,1,0:T(8,128)} subtract(f32[2,5,4,8,128]{4,3,2,1,0:T(8,128)S(1)} %copy-done, f32[2,5,4,8,128]{4,3,2,1,0:T(8,128)S(1)} %sweeps.1) | non-fusion elementwise | flops 40960 | bytes 491520 | tf_op jit(solution)/shard_map/sub | solution.py:414
Async XLA Ops:
  0.0 48.8 %copy-start = (f32[2,5,4,8,128]{4,3,2,1,0:T(8,128)S(1)}, f32[2,5,4,8,128]{4,3,2,1,0:T(8,128)}, u32[]{:S(2)}) copy-start(f32[2,5,4,8,128]{4,3,2,1,0:T(8,128)} %a_hbm.1) | copy-start | bytes 491524
